TPU v7x, 32 devices: a whole 2x2x4 slice. The times are simulated.
32 devices in a mesh: src: 4 (over z), delay: 8 (over y, x, core).
Axes of the slice: x: 2, y: 2, z: 4, core: 2. Of those that a mesh axis runs over, the one named last changes fastest.
Arguments:
- history: float32 [32, 16, 16, 128], P('delay', 'src'), may hold values from -6 to 6
- slot_map: int32 [32], P('delay'), may hold values from 0 to 3, as said below
- interaction: float32 [1536, 128, 128], P(('src', 'delay')), may hold values from -0.0546875 to 0.0546875
- pattern: int32 [3, 1536], P(None, ('src', 'delay')), may hold values from 0 to 15, as said below
- live: int32 [32], P(('src', 'delay')), may hold values from 12 to 48
- near_inverse: float32 [16, 128, 128], P('src'), may hold values from -0.5 to 0.5
- incident: float32 [4, 16, 16, 128], P(None, 'src'), may hold values from -6 to 6
Outputs:
- currents: float32 [4, 16, 16, 128], P(None, 'src')
Inputs may be any that keep to these rules, and one draw needn't show every extreme that they name: `slot_map`: each band's 4 entries are a cyclic rotation of 0 .. 3. `pattern`: row 0 lies in 0 .. 3, row 1 in 0 .. 15, row 2 in 0 .. 3.
All inputs are finite; a program needn't handle non-finite values.
Results may differ from a plain program's by a relative error of at most 0.0003.
Values sent between devices are 32-bit elements; how exact they have to be, the bound alone decides.
No kernel may reach another device: no remote copies, remote signals or barrier semaphores. Data moves between devices by JAX's collectives and lax.ppermute only.
A program may use at most 64 MiB of HBM per device.

v0:
```python
import jax
import jax.numpy as jnp
from jax import lax
from jax.sharding import PartitionSpec as P


def shifted(x, axis, by):
    devices = lax.axis_size(axis)
    pairs = [(i, i + by) for i in range(devices) if 0 <= i + by < devices]
    return lax.ppermute(x, axis, pairs)


def slot_holding(slot_map, wanted, moment):
    length = slot_map.shape[0]
    positions = jnp.arange(length, dtype=jnp.int32)
    return jnp.sum(jnp.where((slot_map + moment) % length == wanted, positions, 0))


def body(history, slot_map, interaction, pattern, live, near_inverse, incident):
    slot_count = history.shape[0]
    group_blocks = history.shape[1]
    columns = history.shape[2]
    block_width = history.shape[3]
    moments = incident.shape[0]
    pair_count = interaction.shape[0]
    positions = jnp.arange(slot_count, dtype=jnp.int32)
    at_front = lax.axis_index("delay") == 0
    in_use = (jnp.arange(pair_count, dtype=jnp.int32) < live[0]).astype(jnp.float32)
    row_match = pattern[0][None, :] == jnp.arange(group_blocks, dtype=jnp.int32)[:, None]
    selector = row_match.astype(jnp.float32) * in_use[None, :]
    band_state = lax.all_gather(history, "src", axis=1, tiled=True)
    results = []
    newest = None
    for moment in range(moments):
        if moment > 0:
            vacated = slot_holding(slot_map, slot_count - 1, moment - 1)
            outgoing_slot = lax.dynamic_index_in_dim(band_state, vacated, 0, keepdims=False)
            incoming = shifted(outgoing_slot, "delay", 1)
            entering = jnp.where(at_front, newest, incoming)
            band_state = lax.dynamic_update_index_in_dim(band_state, entering, vacated, 0)
        holder_match = (slot_map[None, :] + moment) % slot_count == pattern[2][:, None]
        holder = jnp.sum(jnp.where(holder_match, positions[None, :], 0), axis=1)
        picked = band_state[holder, pattern[1]]
        products = jnp.einsum("pab,prb->pra", interaction, picked, precision=lax.Precision.HIGHEST)
        partial_field = jnp.dot(
            selector,
            products.reshape(pair_count, columns * block_width),
            precision=lax.Precision.HIGHEST,
        )
        partial_field = partial_field.reshape(group_blocks, columns, block_width)
        field_sum = lax.psum(partial_field, "delay")
        current = jnp.einsum(
            "iab,irb->ira",
            near_inverse,
            incident[moment] - field_sum,
            precision=lax.Precision.HIGHEST,
        )
        results.append(current)
        if moment + 1 < moments:
            newest = lax.all_gather(current, "src", axis=0, tiled=True)
    return jnp.stack(results)


def solution(mesh):
    return jax.shard_map(
        body,
        mesh=mesh,
        in_specs=(
            P("delay", "src", None, None),
            P("delay"),
            P(("src", "delay"), None, None),
            P(None, ("src", "delay")),
            P(("src", "delay")),
            P("src", None, None),
            P(None, "src", None, None),
        ),
        out_specs=P(None, "src", None, None),
        check_vma=False,
    )
```

profile of v0, /device:TPU:4, one launch (start us, length us, event | category | flops | bytes accessed | tf_op | source)
XLA Modules:
  0.0 216.7 jit_solution(3523601571943106550)
XLA Ops:
  0.0 1.5 fusion.45
  1.5 18.1 %all_gather.12 = f32[4,16,16,128]{3,2,1,0:T(8,128)} all-gather(f32[4,4,16,128]{3,2,1,0:T(8,128)} %param.7), channel_id=1, replica_groups=mesh['src'=4,'delay'=8] {'src'}, dimensions={1}, use_global_device_ids=true | all-gather | bytes 655360 | tf_op jit(solution)/shard_map/all_gather | solution.py:31
  21.5 1.6 dynamic-slice_bitcast_fusion.2
  23.1 1.9 collective-permute-start
  25.0 0.8 slice_bitcast_fusion.1
  25.9 0.7 fusion.64
  26.6 2.6 %gather_fusion = f32[48,16,128]{2,1,0:T(8,128)} fusion(f32[4,16,16,128]{3,2,1,0:T(8,128)} %all_gather.12, s32[48]{0:T(128)S(1)} %get-tuple-element.25), kind=kCustom, calls=%fused_computation | custom fusion | bytes 786816 | tf_op jit(solution)/shard_map/gather | solution.py:43
  29.9 6.0 %fusion.74 = f32[48,16,128]{2,1,0:T(8,128)S(1)} fusion(f32[48,16,128]{2,1,0:T(8,128)} %gather_fusion, f32[48,128,128]{2,1,0:T(8,128)S(1)} %copy-done), kind=kOutput, calls=%fused_computation.121 | convolution fusion | flops 150994944 | bytes 3932160 | tf_op jit(solution)/shard_map/pab,prb->pra/dot_general | solution.py:44
  36.3 24.8 %psum.28 = f32[4,16,128]{2,0,1:T(4,128)S(1)} all-reduce(f32[4,16,128]{2,0,1:T(4,128)S(1)} %fusion.9), channel_id=1, replica_groups=mesh['src'=4,'delay'=8] {'delay'}, use_global_device_ids=true, to_apply=%region_1.2 | all-reduce | flops 8192 | bytes 65536 | tf_op jit(solution)/shard_map/psum | solution.py:51
  61.1 1.4 fusion.73
  66.7 13.4 %all_gather.13 = f32[16,16,128]{2,1,0:T(8,128)S(1)} all-gather(f32[4,16,128]{2,1,0:T(8,128)S(1)} %fusion.21), channel_id=1, replica_groups=mesh['src'=4,'delay'=8] {'src'}, dimensions={0}, use_global_device_ids=true | all-gather | bytes 163840 | tf_op jit(solution)/shard_map/all_gather | solution.py:60
  80.0 1.6 bitcast_dynamic-update-slice_fusion.2
  81.6 2.6 %gather_fusion.1 = f32[48,16,128]{2,1,0:T(8,128)} fusion(f32[4,16,16,128]{3,2,1,0:T(8,128)} %bitcast_dynamic-update-slice_fusion.2, s32[48]{0:T(128)S(1)} %get-tuple-element.24), kind=kCustom, calls=%fused_computation.1 | custom fusion | bytes 786816 | tf_op jit(solution)/shard_map/gather | solution.py:43
  84.3 6.0 %fusion.75 = f32[48,16,128]{2,1,0:T(8,128)S(1)} fusion(f32[48,16,128]{2,1,0:T(8,128)} %gather_fusion.1, f32[48,128,128]{2,1,0:T(8,128)S(1)} %copy-done), kind=kOutput, calls=%fused_computation.122 | convolution fusion | flops 150994944 | bytes 3932160 | tf_op jit(solution)/shard_map/pab,prb->pra/dot_general | solution.py:44
  90.2 1.0 fusion.6
  91.3 22.9 %psum.29 = f32[4,16,128]{2,0,1:T(4,128)S(1)} all-reduce(f32[4,16,128]{2,0,1:T(4,128)} %fusion.6), channel_id=1, replica_groups=mesh['src'=4,'delay'=8] {'delay'}, use_global_device_ids=true, to_apply=%region_4.5 | all-reduce | flops 8192 | bytes 65536 | tf_op jit(solution)/shard_map/psum | solution.py:51
  114.2 0.9 dynamic-slice_bitcast_fusion.1
  115.1 1.9 collective-permute-start.1
  117.6 13.9 %all_gather.14 = f32[16,16,128]{2,1,0:T(8,128)S(1)} all-gather(f32[4,16,128]{2,1,0:T(8,128)S(1)} %fusion.19), channel_id=1, replica_groups=mesh['src'=4,'delay'=8] {'src'}, dimensions={0}, use_global_device_ids=true | all-gather | bytes 163840 | tf_op jit(solution)/shard_map/all_gather | solution.py:60
  132.1 2.6 %gather_fusion.2 = f32[48,16,128]{2,1,0:T(8,128)} fusion(f32[4,16,16,128]{3,2,1,0:T(8,128)} %bitcast_dynamic-update-slice_fusion.1, s32[48]{0:T(128)S(1)} %get-tuple-element.23), kind=kCustom, calls=%fused_computation.2 | custom fusion | bytes 786816 | tf_op jit(solution)/shard_map/gather | solution.py:43
  134.7 6.0 %fusion.76 = f32[48,16,128]{2,1,0:T(8,128)S(1)} fusion(f32[48,16,128]{2,1,0:T(8,128)} %gather_fusion.2, f32[48,128,128]{2,1,0:T(8,128)S(1)} %copy-done), kind=kOutput, calls=%fused_computation.123 | convolution fusion | flops 150994944 | bytes 3932160 | tf_op jit(solution)/shard_map/pab,prb->pra/dot_general | solution.py:44
  140.7 1.0 fusion.3
  141.7 22.9 %psum.30 = f32[4,16,128]{2,0,1:T(4,128)S(1)} all-reduce(f32[4,16,128]{2,0,1:T(4,128)} %fusion.3), channel_id=1, replica_groups=mesh['src'=4,'delay'=8] {'delay'}, use_global_device_ids=true, to_apply=%region_7.8 | all-reduce | flops 8192 | bytes 65536 | tf_op jit(solution)/shard_map/psum | solution.py:51
  164.6 0.9 dynamic-slice_bitcast_fusion
  165.6 1.9 collective-permute-start.2
  168.0 13.5 %all_gather.15 = f32[16,16,128]{2,1,0:T(8,128)S(1)} all-gather(f32[4,16,128]{2,1,0:T(8,128)S(1)} %fusion.17), channel_id=1, replica_groups=mesh['src'=4,'delay'=8] {'src'}, dimensions={0}, use_global_device_ids=true | all-gather | bytes 163840 | tf_op jit(solution)/shard_map/all_gather | solution.py:60
  182.2 2.6 %gather_fusion.3 = f32[48,16,128]{2,1,0:T(8,128)} fusion(f32[4,16,16,128]{3,2,1,0:T(8,128)} %bitcast_dynamic-update-slice_fusion, s32[48]{0:T(128)S(1)} %get-tuple-element.9), kind=kCustom, calls=%fused_computation.3 | custom fusion | bytes 786816 | tf_op jit(solution)/shard_map/gather | solution.py:43
  184.9 6.0 %fusion.77 = f32[48,16,128]{2,1,0:T(8,128)S(1)} fusion(f32[48,16,128]{2,1,0:T(8,128)} %gather_fusion.3, f32[48,128,128]{2,1,0:T(8,128)S(1)} %copy-done), kind=kOutput, calls=%fused_computation.124 | convolution fusion | flops 150994944 | bytes 3932160 | tf_op jit(solution)/shard_map/pab,prb->pra/dot_general | solution.py:44
  190.8 1.0 fusion
  191.9 22.9 %psum.31 = f32[4,16,128]{2,0,1:T(4,128)S(1)} all-reduce(f32[4,16,128]{2,0,1:T(4,128)} %fusion), channel_id=1, replica_groups=mesh['src'=4,'delay'=8] {'delay'}, use_global_device_ids=true, to_apply=%region_10.11 | all-reduce | flops 8192 | bytes 65536 | tf_op jit(solution)/shard_map/psum | solution.py:51
  214.8 0.8 fusion.12
  216.0 0.7 pad_maximum_fusion
  (26 shorter events, 3.9 us)
Async XLA Ops:
  0.0 29.9 %copy-start = (f32[48,128,128]{2,1,0:T(8,128)S(1)}, f32[48,128,128]{2,1,0:T(8,128)}, u32[]{:S(2)}) copy-start(f32[48,128,128]{2,1,0:T(8,128)} %param.9) | copy-start | bytes 9437188
  1.5 61.0 %copy-start.1 = (f32[4,128,128]{2,1,0:T(8,128)S(1)}, f32[4,128,128]{2,1,0:T(8,128)}, u32[]{:S(2)}) copy-start(f32[4,128,128]{2,1,0:T(8,128)} %param.12) | copy-start | bytes 786436
  23.1 56.9 %collective-permute-start = (f32[16,16,128]{2,1,0:T(8,128)}, f32[16,16,128]{2,1,0:T(8,128)}, u32[]{:S(2)}, u32[]{:S(2)}) collective-permute-start(f32[16,16,128]{2,1,0:T(8,128)} %dynamic-slice_bitcast_fusion.2), channel_id=1, source_target_pairs={{0,1},{1,2},{2,3},{3,4},{4,5},{5,6},{6,7},{8,9},{9,10},{10,11},{11... | collective-permute-start | bytes 393224 | tf_op jit(solution)/shard_map/ppermute | solution.py:10
  29.9 6.0 %copy-start.2 = (f32[48]{0:T(128)}, f32[48]{0:T(128)S(1)}, u32[]{:S(2)}) copy-start(f32[48]{0:T(128)S(1)} %compare_convert_fusion) | copy-start | bytes 580
  62.5 27.7 %copy-start.3 = (f32[48]{0:T(128)S(1)}, f32[48]{0:T(128)}, u32[]{:S(2)}) copy-start(f32[48]{0:T(128)} %copy-done.2) | copy-start | bytes 580
  90.2 50.5 %copy-start.4 = (f32[48]{0:T(128)S(1)}, f32[48]{0:T(128)}, u32[]{:S(2)}) copy-start(f32[48]{0:T(128)} %copy-done.2) | copy-start | bytes 580
  115.1 16.3 %collective-permute-start.1 = (f32[16,16,128]{2,1,0:T(8,128)S(1)}, f32[16,16,128]{2,1,0:T(8,128)S(1)}, u32[]{:S(2)}, u32[]{:S(2)}) collective-permute-start(f32[16,16,128]{2,1,0:T(8,128)S(1)} %dynamic-slice_bitcast_fusion.1), channel_id=1, source_target_pairs={{0,1},{1,2},{2,3},{3,4},{4,5},{5,6},{6,7},{8,9},{9,10},{10,11},{11... | collective-permute-start | bytes 393224 | tf_op jit(solution)/shard_map/ppermute | solution.py:10
  165.6 16.0 %collective-permute-start.2 = (f32[16,16,128]{2,1,0:T(8,128)S(1)}, f32[16,16,128]{2,1,0:T(8,128)S(1)}, u32[]{:S(2)}, u32[]{:S(2)}) collective-permute-start(f32[16,16,128]{2,1,0:T(8,128)S(1)} %dynamic-slice_bitcast_fusion), channel_id=1, source_target_pairs={{0,1},{1,2},{2,3},{3,4},{4,5},{5,6},{6,7},{8,9},{9,10},{10,11},{11... | collective-permute-start | bytes 393224 | tf_op jit(solution)/shard_map/ppermute | solution.py:10
where the time goes:
time: 218 us; the launch traced here: 217 us
  blocking collectives  152 us (70%)
  matrix products  29.4 us (13%)
  local copies, waits for them, and re-layouts  16.2 us (7%)
  other arithmetic  6.73 us (3%)
  between operations  6.34 us (3%)
  starting transfers between devices  5.75 us (3%)
    psum x4, blocking collectives, body(): field_sum = lax.psum(partial_field, 'delay')  93.5 us
    all_gather x3, blocking collectives, body(): newest = lax.all_gather(current, 'src', axis=0, tiled=True)  40.7 us
    dot_general x4, matrix products, body(): jnp.einsum('pab,prb->pra', interaction, picked, precision=lax.Precision.H...  23.8 us
    all_gather x1, blocking collectives, body(): band_state = lax.all_gather(history, 'src', axis=1, tiled=True)  18.1 us
    gather x4, local copies, waits for them, and re-layouts, body(): picked = band_state[holder, pattern[1]]  10.6 us
    ppermute x3, starting transfers between devices, shifted(): return lax.ppermute(x, axis, pairs)  5.75 us
  transfers between devices with their start and end apart: 3, of which 0 were waited for; matrix products, arithmetic and copies ran while one was open for 6% of the time, Pallas kernels for 0%

commit v1 on v0

--- a/solution.py
+++ b/solution.py
@@ -28,7 +28,16 @@
     in_use = (jnp.arange(pair_count, dtype=jnp.int32) < live[0]).astype(jnp.float32)
     row_match = pattern[0][None, :] == jnp.arange(group_blocks, dtype=jnp.int32)[:, None]
     selector = row_match.astype(jnp.float32) * in_use[None, :]
-    band_state = lax.all_gather(history, "src", axis=1, tiled=True)
+    ways = lax.axis_size("src")
+    up = [(d, (d + 1) % ways) for d in range(ways)]
+    down = [(d, (d - 1) % ways) for d in range(ways)]
+    earlier, later = ([history], [history])
+    for _ in range(ways // 2):
+        earlier.append(lax.ppermute(earlier[-1], "src", up))
+    for _ in range((ways - 1) // 2):
+        later.append(lax.ppermute(later[-1], "src", down))
+    line = jnp.concatenate([*earlier[::-1], *later[1:]], axis=1)
+    band_state = jnp.roll(line, (lax.axis_index("src") - ways // 2) * history.shape[1], axis=1)
     results = []
     newest = None
     for moment in range(moments):

time: 218 us -> 205 us (0.940)
  blocking collectives: 152 us -> 132 us
  starting transfers between devices: 5.75 us -> 9.64 us
  local copies, waits for them, and re-layouts: 16.2 us -> 19.7 us
    all_gather x1 -> x0, blocking collectives: 18.1 us -> none  [body(): band_state = lax.all_gather(history, 'src', axis=1, tiled=True)]
    ppermute x0 -> x3, starting transfers between devices: none -> 3.88 us  [the longest x1 2.25 us: body(): later.append(lax.ppermute(later[-1], 'src', down))]
    unnamed x10 -> x25, local copies, waits for them, and re-layouts: 0.02 us -> 2.9 us
    psum x4, blocking collectives: 93.5 us -> 90.8 us  [body(): field_sum = lax.psum(partial_field, 'delay')]
  transfers between devices with their start and end apart: 3 -> 6, of which waited for: 0 -> 0; matrix products, arithmetic and copies ran while one was open for 6% -> 4% of each run, Pallas kernels for 0% -> 0%
where the time goes in v1:
time: 205 us; the launch traced here: 204 us
  blocking collectives  132 us (64%)
  matrix products  29.5 us (14%)
  local copies, waits for them, and re-layouts  19.7 us (10%)
  starting transfers between devices  9.64 us (5%)
  between operations  6.72 us (3%)
  other arithmetic  6.28 us (3%)
    psum x4, blocking collectives, body(): field_sum = lax.psum(partial_field, 'delay')  90.8 us
    all_gather x3, blocking collectives, body(): newest = lax.all_gather(current, 'src', axis=0, tiled=True)  41.3 us
    dot_general x4, matrix products, body(): jnp.einsum('pab,prb->pra', interaction, picked, precision=lax.Precision.H...  23.8 us
    gather x4, local copies, waits for them, and re-layouts, body(): picked = band_state[holder, pattern[1]]  10.5 us
    ppermute x3, starting transfers between devices, shifted(): return lax.ppermute(x, axis, pairs)  5.76 us
  transfers between devices with their start and end apart: 6, of which 0 were waited for; matrix products, arithmetic and copies ran while one was open for 4% of the time, Pallas kernels for 0%

profile of v1, /device:TPU:4, one launch (start us, length us, event | category | flops | bytes accessed | tf_op | source)
XLA Modules:
  0.0 203.9 jit_solution(16368991288670428130)
XLA Ops:
  0.0 1.6 collective-permute-start
  1.6 2.2 %collective-permute-start.2 = (f32[4,4,16,128]{3,2,1,0:T(8,128)}, f32[4,4,16,128]{3,2,1,0:T(8,128)S(1)}, u32[]{:S(2)}, u32[]{:S(2)}) collective-permute-start(f32[4,4,16,128]{3,2,1,0:T(8,128)} %param.7), channel_id=1, source_target_pairs={{0,24},{8,0},{16,8},{24,16},{1,25},{9,1},{17,9},{25,17},{2,26},{10... | collective-permute-start | bytes 393224 | tf_op jit(solution)/shard_map/ppermute | solution.py:38
  3.8 1.4 fusion.45
  5.2 1.3 slice_bitcast_fusion.1
  6.5 1.4 fusion.73
  15.9 0.9 constant_dynamic-update-slice_fusion.5
  16.9 0.9 constant_dynamic-update-slice_fusion.1
  17.9 1.0 copy-done.2
  19.7 2.6 %gather_fusion = f32[48,16,128]{2,1,0:T(8,128)} fusion(f32[4,16,16,128]{3,2,1,0:T(8,128)} %constant_dynamic-slice_fusion, s32[48]{0:T(128)S(1)} %get-tuple-element.25), kind=kCustom, calls=%fused_computation | custom fusion | bytes 786816 | tf_op jit(solution)/shard_map/gather | solution.py:52
  22.3 6.0 %fusion.74 = f32[48,16,128]{2,1,0:T(8,128)S(1)} fusion(f32[48,16,128]{2,1,0:T(8,128)} %gather_fusion, f32[48,128,128]{2,1,0:T(8,128)S(1)} %copy-done), kind=kOutput, calls=%fused_computation.130 | convolution fusion | flops 150994944 | bytes 3932160 | tf_op jit(solution)/shard_map/pab,prb->pra/dot_general | solution.py:53
  28.7 22.6 %psum.28 = f32[4,16,128]{2,0,1:T(4,128)S(1)} all-reduce(f32[4,16,128]{2,0,1:T(4,128)S(1)} %fusion.9), channel_id=1, replica_groups=mesh['src'=4,'delay'=8] {'delay'}, use_global_device_ids=true, to_apply=%region_1.2 | all-reduce | flops 8192 | bytes 65536 | tf_op jit(solution)/shard_map/psum | solution.py:60
  51.3 0.9 dynamic-slice_bitcast_fusion.2
  52.2 1.9 collective-permute-start.3
  54.7 14.4 %all_gather.9 = f32[16,16,128]{2,1,0:T(8,128)S(1)} all-gather(f32[4,16,128]{2,1,0:T(8,128)S(1)} %fusion.21), channel_id=1, replica_groups=mesh['src'=4,'delay'=8] {'src'}, dimensions={0}, use_global_device_ids=true | all-gather | bytes 163840 | tf_op jit(solution)/shard_map/all_gather | solution.py:69
  69.8 2.6 %gather_fusion.1 = f32[48,16,128]{2,1,0:T(8,128)} fusion(f32[4,16,16,128]{3,2,1,0:T(8,128)} %bitcast_dynamic-update-slice_fusion.2, s32[48]{0:T(128)S(1)} %get-tuple-element.24), kind=kCustom, calls=%fused_computation.1 | custom fusion | bytes 786816 | tf_op jit(solution)/shard_map/gather | solution.py:52
  72.4 6.0 %fusion.75 = f32[48,16,128]{2,1,0:T(8,128)S(1)} fusion(f32[48,16,128]{2,1,0:T(8,128)} %gather_fusion.1, f32[48,128,128]{2,1,0:T(8,128)S(1)} %copy-done), kind=kOutput, calls=%fused_computation.131 | convolution fusion | flops 150994944 | bytes 3932160 | tf_op jit(solution)/shard_map/pab,prb->pra/dot_general | solution.py:53
  78.3 1.2 fusion.6
  79.5 22.3 %psum.29 = f32[4,16,128]{2,0,1:T(4,128)S(1)} all-reduce(f32[4,16,128]{2,0,1:T(4,128)S(1)} %fusion.6), channel_id=1, replica_groups=mesh['src'=4,'delay'=8] {'delay'}, use_global_device_ids=true, to_apply=%region_4.5 | all-reduce | flops 8192 | bytes 65536 | tf_op jit(solution)/shard_map/psum | solution.py:60
  101.9 0.9 dynamic-slice_bitcast_fusion.1
  102.8 1.9 collective-permute-start.4
  105.3 13.5 %all_gather.10 = f32[16,16,128]{2,1,0:T(8,128)S(1)} all-gather(f32[4,16,128]{2,1,0:T(8,128)S(1)} %fusion.19), channel_id=1, replica_groups=mesh['src'=4,'delay'=8] {'src'}, dimensions={0}, use_global_device_ids=true | all-gather | bytes 163840 | tf_op jit(solution)/shard_map/all_gather | solution.py:69
  119.5 2.6 %gather_fusion.2 = f32[48,16,128]{2,1,0:T(8,128)} fusion(f32[4,16,16,128]{3,2,1,0:T(8,128)} %bitcast_dynamic-update-slice_fusion.1, s32[48]{0:T(128)S(1)} %get-tuple-element.23), kind=kCustom, calls=%fused_computation.2 | custom fusion | bytes 786816 | tf_op jit(solution)/shard_map/gather | solution.py:52
  122.1 6.0 %fusion.76 = f32[48,16,128]{2,1,0:T(8,128)S(1)} fusion(f32[48,16,128]{2,1,0:T(8,128)} %gather_fusion.2, f32[48,128,128]{2,1,0:T(8,128)S(1)} %copy-done), kind=kOutput, calls=%fused_computation.132 | convolution fusion | flops 150994944 | bytes 3932160 | tf_op jit(solution)/shard_map/pab,prb->pra/dot_general | solution.py:53
  128.1 1.0 fusion.3
  129.1 22.9 %psum.30 = f32[4,16,128]{2,0,1:T(4,128)S(1)} all-reduce(f32[4,16,128]{2,0,1:T(4,128)} %fusion.3), channel_id=1, replica_groups=mesh['src'=4,'delay'=8] {'delay'}, use_global_device_ids=true, to_apply=%region_7.8 | all-reduce | flops 8192 | bytes 65536 | tf_op jit(solution)/shard_map/psum | solution.py:60
  152.0 0.9 dynamic-slice_bitcast_fusion
  152.9 1.9 collective-permute-start.5
  155.4 13.4 %all_gather.11 = f32[16,16,128]{2,1,0:T(8,128)S(1)} all-gather(f32[4,16,128]{2,1,0:T(8,128)S(1)} %fusion.17), channel_id=1, replica_groups=mesh['src'=4,'delay'=8] {'src'}, dimensions={0}, use_global_device_ids=true | all-gather | bytes 163840 | tf_op jit(solution)/shard_map/all_gather | solution.py:69
  169.4 2.6 %gather_fusion.3 = f32[48,16,128]{2,1,0:T(8,128)} fusion(f32[4,16,16,128]{3,2,1,0:T(8,128)} %bitcast_dynamic-update-slice_fusion, s32[48]{0:T(128)S(1)} %get-tuple-element.9), kind=kCustom, calls=%fused_computation.3 | custom fusion | bytes 786816 | tf_op jit(solution)/shard_map/gather | solution.py:52
  172.0 6.0 %fusion.77 = f32[48,16,128]{2,1,0:T(8,128)S(1)} fusion(f32[48,16,128]{2,1,0:T(8,128)} %gather_fusion.3, f32[48,128,128]{2,1,0:T(8,128)S(1)} %copy-done), kind=kOutput, calls=%fused_computation.133 | convolution fusion | flops 150994944 | bytes 3932160 | tf_op jit(solution)/shard_map/pab,prb->pra/dot_general | solution.py:53
  178.0 1.0 fusion
  179.0 22.9 %psum.31 = f32[4,16,128]{2,0,1:T(4,128)S(1)} all-reduce(f32[4,16,128]{2,0,1:T(4,128)} %fusion), channel_id=1, replica_groups=mesh['src'=4,'delay'=8] {'delay'}, use_global_device_ids=true, to_apply=%region_10.11 | all-reduce | flops 8192 | bytes 65536 | tf_op jit(solution)/shard_map/psum | solution.py:60
  (48 shorter events, 8.4 us)
Async XLA Ops:
  0.0 22.3 %copy-start = (f32[48,128,128]{2,1,0:T(8,128)S(1)}, f32[48,128,128]{2,1,0:T(8,128)}, u32[]{:S(2)}) copy-start(f32[48,128,128]{2,1,0:T(8,128)} %param.9) | copy-start | bytes 9437188
  0.0 8.7 %collective-permute-start = (f32[4,4,16,128]{3,2,1,0:T(8,128)}, f32[4,4,16,128]{3,2,1,0:T(8,128)S(1)}, u32[]{:S(2)}, u32[]{:S(2)}) collective-permute-start(f32[4,4,16,128]{3,2,1,0:T(8,128)} %param.7), channel_id=1, source_target_pairs={{0,8},{8,16},{16,24},{24,0},{1,9},{9,17},{17,25},{25,1},{2,10},{10... | collective-permute-start | bytes 393224 | tf_op jit(solution)/shard_map/ppermute | solution.py:36
  1.6 15.2 %collective-permute-start.2 = (f32[4,4,16,128]{3,2,1,0:T(8,128)}, f32[4,4,16,128]{3,2,1,0:T(8,128)S(1)}, u32[]{:S(2)}, u32[]{:S(2)}) collective-permute-start(f32[4,4,16,128]{3,2,1,0:T(8,128)} %param.7), channel_id=1, source_target_pairs={{0,24},{8,0},{16,8},{24,16},{1,25},{9,1},{17,9},{25,17},{2,26},{10... | collective-permute-start | bytes 393224 | tf_op jit(solution)/shard_map/ppermute | solution.py:38
  8.7 7.2 %collective-permute-start.1 = (f32[4,4,16,128]{3,2,1,0:T(8,128)S(1)}, f32[4,4,16,128]{3,2,1,0:T(8,128)S(1)}, u32[]{:S(2)}, u32[]{:S(2)}) collective-permute-start(f32[4,4,16,128]{3,2,1,0:T(8,128)S(1)} %collective-permute-done), channel_id=1, source_target_pairs={{0,8},{8,16},{16,24},{24,0},{1,9},{9,17},{17,25},{25,1},{2,10},{10... | collective-permute-start | bytes 393224 | tf_op jit(solution)/shard_map/ppermute | solution.py:36
  16.9 11.4 %copy-start.6 = (s32[48]{0:T(128)S(1)}, s32[48]{0:T(128)}, u32[]{:S(2)}) copy-start(s32[48]{0:T(128)} %get-tuple-element.21) | copy-start | bytes 580
  16.9 11.4 %copy-start.7 = (f32[48]{0:T(128)S(1)}, f32[48]{0:T(128)}, u32[]{:S(2)}) copy-start(f32[48]{0:T(128)} %compare_convert_fusion) | copy-start | bytes 580
  17.9 1.0 copy-start.2
  18.8 35.3 %copy-start.5 = (f32[1,4,16,128]{3,2,1,0:T(8,128)S(1)}, f32[1,4,16,128]{3,2,1,0:T(8,128)}, u32[]{:S(2)}) copy-start(f32[1,4,16,128]{3,2,1,0:T(8,128)} %get-tuple-element.20) | copy-start | bytes 98308
  18.8 35.4 %copy-start.1 = (f32[4,128,128]{2,1,0:T(8,128)S(1)}, f32[4,128,128]{2,1,0:T(8,128)}, u32[]{:S(2)}) copy-start(f32[4,128,128]{2,1,0:T(8,128)} %param.12) | copy-start | bytes 786436
  52.2 16.9 %collective-permute-start.3 = (f32[16,16,128]{2,1,0:T(8,128)S(1)}, f32[16,16,128]{2,1,0:T(8,128)S(1)}, u32[]{:S(2)}, u32[]{:S(2)}) collective-permute-start(f32[16,16,128]{2,1,0:T(8,128)S(1)} %dynamic-slice_bitcast_fusion.2), channel_id=1, source_target_pairs={{0,1},{1,2},{2,3},{3,4},{4,5},{5,6},{6,7},{8,9},{9,10},{10,11},{11... | collective-permute-start | bytes 393224 | tf_op jit(solution)/shard_map/ppermute | solution.py:10
  54.2 50.5 %copy-start.4 = (f32[1,4,16,128]{3,2,1,0:T(8,128)S(1)}, f32[1,4,16,128]{3,2,1,0:T(8,128)}, u32[]{:S(2)}) copy-start(f32[1,4,16,128]{3,2,1,0:T(8,128)} %get-tuple-element.19) | copy-start | bytes 98308
  78.3 49.7 %copy-start.8 = (f32[48]{0:T(128)S(1)}, f32[48]{0:T(128)}, u32[]{:S(2)}) copy-start(f32[48]{0:T(128)} %compare_convert_fusion) | copy-start | bytes 580
  102.8 16.0 %collective-permute-start.4 = (f32[16,16,128]{2,1,0:T(8,128)S(1)}, f32[16,16,128]{2,1,0:T(8,128)S(1)}, u32[]{:S(2)}, u32[]{:S(2)}) collective-permute-start(f32[16,16,128]{2,1,0:T(8,128)S(1)} %dynamic-slice_bitcast_fusion.1), channel_id=1, source_target_pairs={{0,1},{1,2},{2,3},{3,4},{4,5},{5,6},{6,7},{8,9},{9,10},{10,11},{11... | collective-permute-start | bytes 393224 | tf_op jit(solution)/shard_map/ppermute | solution.py:10
  104.8 50.1 %copy-start.3 = (f32[1,4,16,128]{3,2,1,0:T(8,128)S(1)}, f32[1,4,16,128]{3,2,1,0:T(8,128)}, u32[]{:S(2)}) copy-start(f32[1,4,16,128]{3,2,1,0:T(8,128)} %get-tuple-element.18) | copy-start | bytes 98308
  152.9 15.8 %collective-permute-start.5 = (f32[16,16,128]{2,1,0:T(8,128)S(1)}, f32[16,16,128]{2,1,0:T(8,128)S(1)}, u32[]{:S(2)}, u32[]{:S(2)}) collective-permute-start(f32[16,16,128]{2,1,0:T(8,128)S(1)} %dynamic-slice_bitcast_fusion), channel_id=1, source_target_pairs={{0,1},{1,2},{2,3},{3,4},{4,5},{5,6},{6,7},{8,9},{9,10},{10,11},{11... | collective-permute-start | bytes 393224 | tf_op jit(solution)/shard_map/ppermute | solution.py:10
